TPU v7x, 128 devices: a whole 4x4x4 slice. The times are simulated.
128 devices in a mesh: own: 16 (over y, z), red: 8 (over x, core).
Axes of the slice: x: 4, y: 4, z: 4, core: 2. Of those that a mesh axis runs over, the one named last changes fastest.
Arguments:
- amp_tiles: bfloat16 [8192, 128, 128], P(('own', 'red')), may hold values from -6 to 6
- int_tiles: bfloat16 [8192, 128, 128], P(('own', 'red')), may hold values from -0.0625 to 0.0625
- requests: int32 [16, 8, 16, 2, 8], P('own', 'red'), may hold values from -1 to 63, as said below
- tri_amp: int32 [512, 8, 64], P('own', 'red'), may hold values from 0 to 127, as said below
- tri_int: int32 [512, 8, 64], P('own', 'red'), may hold values from 0 to 127, as said below
- tri_count: int32 [512, 8], P('own', 'red'), may hold values from 1 to 64, as said below
Outputs:
- residual: float32 [512, 128, 128], P(('own', 'red'))
Inputs may be any that keep to these rules, and one draw needn't show every extreme that they name: -1 marks an empty slot and live slots come first; the live numbers in one row of 8 slots are distinct; every owner device has 8 live amplitude requests to some holder and 8 live integral requests to some holder. tri_amp[t, r, k] // 8 is a holder h and tri_amp[t, r, k] % 8 is below the number of live amplitude requests of the owner of t, on red index r, to h. `tri_int`: likewise for the integral requests. `tri_count`: on every owner and red index some residual tile has 64 live triples.
All inputs are finite; a program needn't handle non-finite values.
Results may differ from a plain program's by a relative error of at most 0.0003.
Values may be sent and summed in bfloat16 or wider, within the bound.
No kernel may reach another device: no remote copies, remote signals or barrier semaphores. Data moves between devices by JAX's collectives and lax.ppermute only.
A program may use at most 128 MiB of HBM per device.

v0:
```python
import math
import jax
import jax.numpy as jnp
from jax import lax
from jax.sharding import PartitionSpec as P


def select_tiles(store, wanted):
    clipped = jnp.clip(wanted, 0, store.shape[0] - 1)
    picked = store[clipped]
    return jnp.where((wanted >= 0)[:, :, None, None], picked, jnp.zeros((), store.dtype))


def contract_rows(got_amp, got_int, amp_pos, int_pos, counts):
    row_count, slot_count = amp_pos.shape
    received = got_amp.shape[0]
    tile_width = got_amp.shape[-1]
    block_rows = math.gcd(8, row_count)
    keep_mask = lax.broadcasted_iota(jnp.int32, (row_count, slot_count), 1) < counts[:, None]
    flat_amp = got_amp.reshape(received, tile_width * tile_width)
    flat_int = got_int.reshape(received, tile_width * tile_width)
    slot_iota = lax.broadcasted_iota(jnp.int32, (1, 1, received), 2)

    def one_block(operands):
        block_amp, block_int, block_keep = operands
        pick_amp = ((block_amp[:, :, None] == slot_iota) & block_keep[:, :, None]).astype(
            got_amp.dtype
        )
        pick_int = (block_int[:, :, None] == slot_iota).astype(got_int.dtype)
        left_tiles = jnp.einsum(
            "nkm,mx->nkx", pick_amp, flat_amp, preferred_element_type=jnp.float32
        ).astype(got_amp.dtype)
        right_tiles = jnp.einsum(
            "nkm,mx->nkx", pick_int, flat_int, preferred_element_type=jnp.float32
        ).astype(got_int.dtype)
        left_tiles = left_tiles.reshape(block_rows, slot_count, tile_width, tile_width)
        right_tiles = right_tiles.reshape(block_rows, slot_count, tile_width, tile_width)
        return jnp.einsum(
            "nkpc,nkqc->npq", left_tiles, right_tiles, preferred_element_type=jnp.float32
        )

    def in_blocks(values):
        return values.reshape((row_count // block_rows, block_rows) + values.shape[1:])

    product = lax.map(one_block, (in_blocks(amp_pos), in_blocks(int_pos), in_blocks(keep_mask)))
    return product.reshape(row_count, tile_width, tile_width)


def body(amp_tiles, int_tiles, requests, tri_amp, tri_int, tri_count):
    wanted = requests[0, 0]
    asked = lax.all_to_all(wanted, "own", split_axis=0, concat_axis=0, tiled=True)
    send_amp = select_tiles(amp_tiles, asked[:, 0])
    send_int = select_tiles(int_tiles, asked[:, 1])
    got_amp, got_int = (
        lax.all_to_all(send_amp, "own", split_axis=0, concat_axis=0, tiled=True),
        lax.all_to_all(send_int, "own", split_axis=0, concat_axis=0, tiled=True),
    )
    flat_amp = got_amp.reshape((-1,) + got_amp.shape[2:])
    flat_int = got_int.reshape((-1,) + got_int.shape[2:])
    amp_pos = tri_amp[:, 0]
    int_pos = tri_int[:, 0]
    counts = tri_count[:, 0]
    share = amp_pos.shape[0] // lax.axis_size("red")
    partial_sum = contract_rows(flat_amp, flat_int, amp_pos, int_pos, counts)
    total_sum = lax.psum(partial_sum, "red")
    return lax.dynamic_slice_in_dim(total_sum, lax.axis_index("red") * share, share, 0)


def solution(mesh):
    placed = (
        P(("own", "red"), None, None),
        P(("own", "red"), None, None),
        P("own", "red", None, None, None),
        P("own", "red", None),
        P("own", "red", None),
        P("own", "red"),
    )
    return jax.shard_map(
        body, mesh=mesh, in_specs=placed, out_specs=P(("own", "red"), None, None), check_vma=False
    )
```

profile of v0, /device:TPU:0, one launch (start us, length us, event | category | flops | bytes accessed | tf_op | source)
XLA Modules:
  0.0 401.2 jit_solution(17868745536821819180)
XLA Ops:
  7.5 15.6 %all_to_all.15 = s32[16,2,8]{2,1,0:T(2,128)S(1)} all-to-all(s32[16,2,8]{2,1,0:T(2,128)S(1)} %bitcast.88), channel_id=1, replica_groups=mesh['own'=16,'red'=8] {'own'}, dimensions={0} | all-to-all | bytes 2048 | tf_op jit(solution)/shard_map/all_to_all | solution.py:51
  23.4 3.0 gather_fusion.1
  26.4 6.9 %copy_select_fusion = bf16[16,8,128,128]{3,1,2,0:T(8,128)(2,1)} fusion(bf16[16,8,128,128]{3,2,1,0:T(8,128)(2,1)} %bitcast.85, pred[16,8]{1,0:T(8,128)(4,1)S(1)} %copy.25), kind=kLoop, calls=%fused_computation.21 | loop fusion | flops 2097152 | bytes 8388736 | tf_op jit(solution)/shard_map/jit(_where)/select_n | solution.py:11
  33.3 4.7 %all-to-all-start.2 = ((bf16[16,8,128,128]{3,1,2,0:T(8,128)(2,1)}), bf16[16,8,128,128]{3,1,2,0:T(8,128)(2,1)}, u32[]{:S(2)}, u32[]{:S(2)}) async-start(bf16[16,8,128,128]{3,1,2,0:T(8,128)(2,1)} %copy_select_fusion), calls=%async_computation.2 | async-start | bytes 8388608 | tf_op jit(solution)/shard_map/all_to_all | solution.py:56
  38.3 3.0 gather_fusion
  41.3 6.8 %copy_select_fusion.1 = bf16[16,8,128,128]{3,1,2,0:T(8,128)(2,1)} fusion(bf16[16,8,128,128]{3,2,1,0:T(8,128)(2,1)} %bitcast.86, pred[16,8]{1,0:T(8,128)(4,1)S(1)} %copy.21), kind=kLoop, calls=%fused_computation.22 | loop fusion | flops 2097152 | bytes 8388736 | tf_op jit(solution)/shard_map/jit(_where)/select_n | solution.py:11
  48.2 44.4 %all-to-all-done.2 = bf16[16,8,128,128]{3,1,2,0:T(8,128)(2,1)} async-done(((bf16[16,8,128,128]{3,1,2,0:T(8,128)(2,1)}), bf16[16,8,128,128]{3,1,2,0:T(8,128)(2,1)}, u32[]{:S(2)}, u32[]{:S(2)}) %all-to-all-start.2) | async-done | bytes 4194336 | tf_op jit(solution)/shard_map/all_to_all | solution.py:56
  92.6 5.1 %all-to-all-start.1 = ((bf16[16,8,128,128]{3,1,2,0:T(8,128)(2,1)}), bf16[16,8,128,128]{3,1,2,0:T(8,128)(2,1)}, u32[]{:S(2)}, u32[]{:S(2)}) async-start(bf16[16,8,128,128]{3,1,2,0:T(8,128)(2,1)} %copy_select_fusion.1), calls=%async_computation.1 | async-start | bytes 8388608 | tf_op jit(solution)/shard_map/all_to_all | solution.py:55
  99.2 48.2 %all-to-all-done.1 = bf16[16,8,128,128]{3,1,2,0:T(8,128)(2,1)} async-done(((bf16[16,8,128,128]{3,1,2,0:T(8,128)(2,1)}), bf16[16,8,128,128]{3,1,2,0:T(8,128)(2,1)}, u32[]{:S(2)}, u32[]{:S(2)}) %all-to-all-start.1) | async-done | bytes 4194336 | tf_op jit(solution)/shard_map/all_to_all | solution.py:55
  147.4 178.1 %while.12 = (s32[]{:T(128)}, f32[4,8,128,128]{3,2,1,0:T(8,128)}, s32[4,8,64]{2,1,0:T(8,128)}, pred[4,8,64]{2,1,0:T(8,128)(4,1)S(1)}, bf16[128,16384]{1,0:T(8,128...) while((s32[]{:T(128)}, f32[4,8,128,128]{3,2,1,0:T(8,128)}, ...), condition=%wide.region_1.2_spmd.clone.clone, body=%wide.region_0.1_spmd.clone.clone.sunk | while | flops 6459424768 | bytes 143145056 | solution.py:45
  148.1 7.0 %convolution_convert_fusion.5 = bf16[8,64,16384]{2,1,0:T(8,128)(2,1)S(1)} fusion(bf16[128,16384]{1,0:T(8,128)(2,1)} %get-tuple-element.172, s32[8,64]{1,0:T(8,128)S(1)} %get-tuple-element.151, pred[8,64]{1,0:T(8,128)(4,1)S(1)} %dynamic-slice_bitcast_fusion.6), kind=kOutput, calls=%fused_computation.4.clone.1 | convolution fusion | flops 2156003328 | bytes 20974080 | tf_op jit(solution)/shard_map/while/body/eval_jaxpr/nkm,mx->nkx/dot_general | solution.py:30
  155.1 8.3 %copy.38 = bf16[64,8,128,128]{3,2,1,0:T(8,128)(2,1)} copy(bf16[64,8,128,128]{3,1,2,0:T(8,128)(2,1)S(1)} %bitcast.81) | data formatting | bytes 33554432 | tf_op jit(solution)/shard_map/while
  163.4 6.9 %convolution_convert_fusion.4 = bf16[8,64,16384]{2,1,0:T(8,128)(2,1)S(1)} fusion(bf16[128,16384]{1,0:T(8,128)(2,1)} %get-tuple-element.174, s32[8,64]{1,0:T(8,128)S(1)} %get-tuple-element.150), kind=kOutput, calls=%fused_computation.3.clone.1 | convolution fusion | flops 2155937792 | bytes 20973568 | tf_op jit(solution)/shard_map/while/body/eval_jaxpr/nkm,mx->nkx/dot_general | solution.py:33
  170.3 8.3 %copy.37 = bf16[64,8,128,128]{3,2,1,0:T(8,128)(2,1)} copy(bf16[64,8,128,128]{3,1,2,0:T(8,128)(2,1)S(1)} %bitcast.82) | data formatting | bytes 33554432 | tf_op jit(solution)/shard_map/while
  178.6 13.3 %fusion.30 = f32[4,8,128,128]{3,2,1,0:T(8,128)} fusion(f32[4,8,128,128]{3,2,1,0:T(8,128)} %get-tuple-element.161, s32[]{:T(128)} %get-tuple-element.160, bf16[8,64,128,128]{3,2,1,0:T(8,128)(2,1)} %bitcast.84, bf16[8,64,128,128]{3,2,1,0:T(8,128)(2,1)} %bitcast.83), kind=kOutput, calls=%fused_computation.11.clone.1 | convolution fusion | flops 2147483648 | bytes 34079232 | tf_op jit(solution)/shard_map/while/body/eval_jaxpr/nkpc,nkqc->npq/dot_general | solution.py:38
  192.6 7.0 %convolution_convert_fusion.5 = bf16[8,64,16384]{2,1,0:T(8,128)(2,1)S(1)} fusion(bf16[128,16384]{1,0:T(8,128)(2,1)} %get-tuple-element.172, s32[8,64]{1,0:T(8,128)S(1)} %get-tuple-element.151, pred[8,64]{1,0:T(8,128)(4,1)S(1)} %dynamic-slice_bitcast_fusion.6), kind=kOutput, calls=%fused_computation.4.clone.1 | convolution fusion | flops 2156003328 | bytes 20974080 | tf_op jit(solution)/shard_map/while/body/eval_jaxpr/nkm,mx->nkx/dot_general | solution.py:30
  199.6 8.3 %copy.38 = bf16[64,8,128,128]{3,2,1,0:T(8,128)(2,1)} copy(bf16[64,8,128,128]{3,1,2,0:T(8,128)(2,1)S(1)} %bitcast.81) | data formatting | bytes 33554432 | tf_op jit(solution)/shard_map/while
  207.9 6.9 %convolution_convert_fusion.4 = bf16[8,64,16384]{2,1,0:T(8,128)(2,1)S(1)} fusion(bf16[128,16384]{1,0:T(8,128)(2,1)} %get-tuple-element.174, s32[8,64]{1,0:T(8,128)S(1)} %get-tuple-element.150), kind=kOutput, calls=%fused_computation.3.clone.1 | convolution fusion | flops 2155937792 | bytes 20973568 | tf_op jit(solution)/shard_map/while/body/eval_jaxpr/nkm,mx->nkx/dot_general | solution.py:33
  214.8 8.3 %copy.37 = bf16[64,8,128,128]{3,2,1,0:T(8,128)(2,1)} copy(bf16[64,8,128,128]{3,1,2,0:T(8,128)(2,1)S(1)} %bitcast.82) | data formatting | bytes 33554432 | tf_op jit(solution)/shard_map/while
  223.1 13.3 %fusion.30 = f32[4,8,128,128]{3,2,1,0:T(8,128)} fusion(f32[4,8,128,128]{3,2,1,0:T(8,128)} %get-tuple-element.161, s32[]{:T(128)} %get-tuple-element.160, bf16[8,64,128,128]{3,2,1,0:T(8,128)(2,1)} %bitcast.84, bf16[8,64,128,128]{3,2,1,0:T(8,128)(2,1)} %bitcast.83), kind=kOutput, calls=%fused_computation.11.clone.1 | convolution fusion | flops 2147483648 | bytes 34079232 | tf_op jit(solution)/shard_map/while/body/eval_jaxpr/nkpc,nkqc->npq/dot_general | solution.py:38
  237.2 7.0 %convolution_convert_fusion.5 = bf16[8,64,16384]{2,1,0:T(8,128)(2,1)S(1)} fusion(bf16[128,16384]{1,0:T(8,128)(2,1)} %get-tuple-element.172, s32[8,64]{1,0:T(8,128)S(1)} %get-tuple-element.151, pred[8,64]{1,0:T(8,128)(4,1)S(1)} %dynamic-slice_bitcast_fusion.6), kind=kOutput, calls=%fused_computation.4.clone.1 | convolution fusion | flops 2156003328 | bytes 20974080 | tf_op jit(solution)/shard_map/while/body/eval_jaxpr/nkm,mx->nkx/dot_general | solution.py:30
  244.1 8.3 %copy.38 = bf16[64,8,128,128]{3,2,1,0:T(8,128)(2,1)} copy(bf16[64,8,128,128]{3,1,2,0:T(8,128)(2,1)S(1)} %bitcast.81) | data formatting | bytes 33554432 | tf_op jit(solution)/shard_map/while
  252.4 6.9 %convolution_convert_fusion.4 = bf16[8,64,16384]{2,1,0:T(8,128)(2,1)S(1)} fusion(bf16[128,16384]{1,0:T(8,128)(2,1)} %get-tuple-element.174, s32[8,64]{1,0:T(8,128)S(1)} %get-tuple-element.150), kind=kOutput, calls=%fused_computation.3.clone.1 | convolution fusion | flops 2155937792 | bytes 20973568 | tf_op jit(solution)/shard_map/while/body/eval_jaxpr/nkm,mx->nkx/dot_general | solution.py:33
  259.4 8.3 %copy.37 = bf16[64,8,128,128]{3,2,1,0:T(8,128)(2,1)} copy(bf16[64,8,128,128]{3,1,2,0:T(8,128)(2,1)S(1)} %bitcast.82) | data formatting | bytes 33554432 | tf_op jit(solution)/shard_map/while
  267.7 13.3 %fusion.30 = f32[4,8,128,128]{3,2,1,0:T(8,128)} fusion(f32[4,8,128,128]{3,2,1,0:T(8,128)} %get-tuple-element.161, s32[]{:T(128)} %get-tuple-element.160, bf16[8,64,128,128]{3,2,1,0:T(8,128)(2,1)} %bitcast.84, bf16[8,64,128,128]{3,2,1,0:T(8,128)(2,1)} %bitcast.83), kind=kOutput, calls=%fused_computation.11.clone.1 | convolution fusion | flops 2147483648 | bytes 34079232 | tf_op jit(solution)/shard_map/while/body/eval_jaxpr/nkpc,nkqc->npq/dot_general | solution.py:38
  281.7 7.0 %convolution_convert_fusion.5 = bf16[8,64,16384]{2,1,0:T(8,128)(2,1)S(1)} fusion(bf16[128,16384]{1,0:T(8,128)(2,1)} %get-tuple-element.172, s32[8,64]{1,0:T(8,128)S(1)} %get-tuple-element.151, pred[8,64]{1,0:T(8,128)(4,1)S(1)} %dynamic-slice_bitcast_fusion.6), kind=kOutput, calls=%fused_computation.4.clone.1 | convolution fusion | flops 2156003328 | bytes 20974080 | tf_op jit(solution)/shard_map/while/body/eval_jaxpr/nkm,mx->nkx/dot_general | solution.py:30
  288.7 8.3 %copy.38 = bf16[64,8,128,128]{3,2,1,0:T(8,128)(2,1)} copy(bf16[64,8,128,128]{3,1,2,0:T(8,128)(2,1)S(1)} %bitcast.81) | data formatting | bytes 33554432 | tf_op jit(solution)/shard_map/while
  296.9 6.9 %convolution_convert_fusion.4 = bf16[8,64,16384]{2,1,0:T(8,128)(2,1)S(1)} fusion(bf16[128,16384]{1,0:T(8,128)(2,1)} %get-tuple-element.174, s32[8,64]{1,0:T(8,128)S(1)} %get-tuple-element.150), kind=kOutput, calls=%fused_computation.3.clone.1 | convolution fusion | flops 2155937792 | bytes 20973568 | tf_op jit(solution)/shard_map/while/body/eval_jaxpr/nkm,mx->nkx/dot_general | solution.py:33
  303.9 8.3 %copy.37 = bf16[64,8,128,128]{3,2,1,0:T(8,128)(2,1)} copy(bf16[64,8,128,128]{3,1,2,0:T(8,128)(2,1)S(1)} %bitcast.82) | data formatting | bytes 33554432 | tf_op jit(solution)/shard_map/while
  312.2 13.3 %fusion.30 = f32[4,8,128,128]{3,2,1,0:T(8,128)} fusion(f32[4,8,128,128]{3,2,1,0:T(8,128)} %get-tuple-element.161, s32[]{:T(128)} %get-tuple-element.160, bf16[8,64,128,128]{3,2,1,0:T(8,128)(2,1)} %bitcast.84, bf16[8,64,128,128]{3,2,1,0:T(8,128)(2,1)} %bitcast.83), kind=kOutput, calls=%fused_computation.11.clone.1 | convolution fusion | flops 2147483648 | bytes 34079232 | tf_op jit(solution)/shard_map/while/body/eval_jaxpr/nkpc,nkqc->npq/dot_general | solution.py:38
  325.6 67.1 %all-reduce.2.cloned.1.call-done = f32[32,128,128]{2,1,0:T(8,128)} async-done(((f32[32,128,128]{2,1,0:T(8,128)}), f32[32,128,128]{2,1,0:T(8,128)}) %all-reduce.2.cloned.1.call-update) | async-done | bytes 2097168 | tf_op jit(solution)/shard_map/psum | solution.py:65
  392.7 1.7 constant_dynamic-slice_fusion
  (39 shorter events, 6.0 us)
Async XLA Ops:
  6.5 16.8 %copy-start = (bf16[64,128,128]{2,1,0:T(8,128)(2,1)S(1)}, bf16[64,128,128]{2,1,0:T(8,128)(2,1)}, u32[]{:S(2)}) copy-start(bf16[64,128,128]{2,1,0:T(8,128)(2,1)} %param.9) | copy-start | bytes 6291460
  33.3 5.0 %copy-start.2 = (bf16[64,128,128]{2,1,0:T(8,128)(2,1)S(1)}, bf16[64,128,128]{2,1,0:T(8,128)(2,1)}, u32[]{:S(2)}) copy-start(bf16[64,128,128]{2,1,0:T(8,128)(2,1)} %param.8) | copy-start | bytes 6291460
  33.3 59.3 %all-to-all-start.2 = ((bf16[16,8,128,128]{3,1,2,0:T(8,128)(2,1)}), bf16[16,8,128,128]{3,1,2,0:T(8,128)(2,1)}, u32[]{:S(2)}, u32[]{:S(2)}) async-start(bf16[16,8,128,128]{3,1,2,0:T(8,128)(2,1)} %copy_select_fusion), calls=%async_computation.2 | async-start | bytes 8388608 | tf_op jit(solution)/shard_map/all_to_all | solution.py:56
  48.2 50.3 %copy-start.3 = (s32[32,1]{0,1:T(1,128)S(1)}, s32[32,1]{0,1:T(1,128)}, u32[]{:S(2)}) copy-start(s32[32,1]{0,1:T(1,128)} %param.13) | copy-start | bytes 388
  92.6 54.8 %all-to-all-start.1 = ((bf16[16,8,128,128]{3,1,2,0:T(8,128)(2,1)}), bf16[16,8,128,128]{3,1,2,0:T(8,128)(2,1)}, u32[]{:S(2)}, u32[]{:S(2)}) async-start(bf16[16,8,128,128]{3,1,2,0:T(8,128)(2,1)} %copy_select_fusion.1), calls=%async_computation.1 | async-start | bytes 8388608 | tf_op jit(solution)/shard_map/all_to_all | solution.py:55
  97.7 295.0 %all-reduce.2.cloned.1.call-start = ((), (), s32[]{:S(2)}) async-start(), calls=%async_computation.3 | async-start | bytes 4194304 | tf_op jit(solution)/shard_map/psum | solution.py:65
  325.5 68.8 %copy-start.1 = (bf16[64,128,128]{2,1,0:T(8,128)(2,1)S(1)}, bf16[64,128,128]{2,1,0:T(8,128)(2,1)}, u32[]{:S(2)}) copy-start(bf16[64,128,128]{2,1,0:T(8,128)(2,1)} %param.9) | copy-start | bytes 6291460
Sparse Core Ops, SparseCore 0:
  325.7 66.9 all-reduce.1
where the time goes:
time: 402 us; the launch traced here: 401 us
  waiting for transfers between devices  160 us (40%)
  matrix products  109 us (27%)
  local copies, waits for them, and re-layouts  79 us (20%)
  blocking collectives  15.6 us (4%)
  other arithmetic  14.4 us (4%)
  between operations  13.5 us (3%)
  starting transfers between devices  9.98 us (2%)
    psum x1, waiting for transfers between devices, body(): total_sum = lax.psum(partial_sum, 'red')  67.1 us
    while x8, local copies, waits for them, and re-layouts  66.3 us
    dot_general x4, matrix products, one_block(): jnp.einsum('nkpc,nkqc->npq', left_tiles, right_tiles, preferred_element_t...  53.3 us
    all_to_all x1, waiting for transfers between devices, body(): lax.all_to_all(send_amp, 'own', split_axis=0, concat_axis=0, tiled=True)  48.2 us
    all_to_all x1, waiting for transfers between devices, body(): lax.all_to_all(send_int, 'own', split_axis=0, concat_axis=0, tiled=True)  44.4 us
    dot_general x4, matrix products, one_block(): jnp.einsum('nkm,mx->nkx', pick_amp, flat_amp, preferred_element_type=jnp....  27.9 us
    dot_general x4, matrix products, one_block(): jnp.einsum('nkm,mx->nkx', pick_int, flat_int, preferred_element_type=jnp....  27.8 us
    all_to_all x1, blocking collectives, body(): lax.all_to_all(wanted, 'own', split_axis=0, concat_axis=0, tiled=True)  15.6 us
  transfers between devices with their start and end apart: 3, of which 3 were waited for; matrix products, arithmetic and copies ran while one was open for 3% of the time, Pallas kernels for 0%

commit v1 on v0

--- a/solution.py
+++ b/solution.py
@@ -62,7 +62,11 @@
     counts = tri_count[:, 0]
     share = amp_pos.shape[0] // lax.axis_size("red")
     partial_sum = contract_rows(flat_amp, flat_int, amp_pos, int_pos, counts)
-    total_sum = lax.psum(partial_sum, "red")
+    total_sum = partial_sum
+    for hop in (1, 2, 4):
+        total_sum = total_sum + lax.ppermute(
+            total_sum, "red", [(dev, dev ^ hop) for dev in range(8)]
+        )
     return lax.dynamic_slice_in_dim(total_sum, lax.axis_index("red") * share, share, 0)
 
 

time: 402 us -> 426 us (1.060)
  waiting for transfers between devices: 160 us -> 189 us
  between operations: 13.5 us -> 0.08 us
  other arithmetic: 14.4 us -> 19.8 us
  starting transfers between devices: 9.98 us -> 14.4 us
    ppermute x0 -> x3, waiting for transfers between devices: none -> 96.2 us  [body(): lax.ppermute(total_sum, 'red', [(dev, dev ^ hop) for dev in range(8)])]
    psum x1 -> x0, waiting for transfers between devices: 67.1 us -> none  [body(): total_sum = lax.psum(partial_sum, 'red')]
    add x0 -> x3, other arithmetic: none -> 5.38 us  [body(): total_sum + lax.ppermute(total_sum, 'red', [(dev, dev ^ hop) for dev in r...]
    ppermute x0 -> x3, starting transfers between devices: none -> 4.59 us  [body(): lax.ppermute(total_sum, 'red', [(dev, dev ^ hop) for dev in range(8)])]
  transfers between devices with their start and end apart: 3 -> 5, of which waited for: 3 -> 5; matrix products, arithmetic and copies ran while one was open for 3% -> 3% of each run, Pallas kernels for 0% -> 0%
where the time goes in v1:
time: 426 us; the launch traced here: 425 us
  waiting for transfers between devices  189 us (44%)
  matrix products  109 us (26%)
  local copies, waits for them, and re-layouts  77.3 us (18%)
  other arithmetic  19.8 us (5%)
  blocking collectives  15.6 us (4%)
  starting transfers between devices  14.4 us (3%)
    ppermute x3, waiting for transfers between devices, body(): lax.ppermute(total_sum, 'red', [(dev, dev ^ hop) for dev in range(8)])  96.2 us
    while x8, local copies, waits for them, and re-layouts  66.2 us
    dot_general x4, matrix products, one_block(): jnp.einsum('nkpc,nkqc->npq', left_tiles, right_tiles, preferred_element_t...  53.3 us
    all_to_all x1, waiting for transfers between devices, body(): lax.all_to_all(send_amp, 'own', split_axis=0, concat_axis=0, tiled=True)  48.4 us
    all_to_all x1, waiting for transfers between devices, body(): lax.all_to_all(send_int, 'own', split_axis=0, concat_axis=0, tiled=True)  44.4 us
    dot_general x4, matrix products, one_block(): jnp.einsum('nkm,mx->nkx', pick_amp, flat_amp, preferred_element_type=jnp....  27.9 us
    dot_general x4, matrix products, one_block(): jnp.einsum('nkm,mx->nkx', pick_int, flat_int, preferred_element_type=jnp....  27.8 us
    all_to_all x1, blocking collectives, body(): lax.all_to_all(wanted, 'own', split_axis=0, concat_axis=0, tiled=True)  15.6 us
  transfers between devices with their start and end apart: 5, of which 5 were waited for; matrix products, arithmetic and copies ran while one was open for 3% of the time, Pallas kernels for 0%

profile of v1, /device:TPU:0, one launch (start us, length us, event | category | flops | bytes accessed | tf_op | source)
XLA Modules:
  0.0 425.1 jit_solution(11494110859733789633)
XLA Ops:
  0.9 15.6 %all_to_all.15 = s32[16,2,8]{2,1,0:T(2,128)S(1)} all-to-all(s32[16,2,8]{2,1,0:T(2,128)S(1)} %bitcast.89), channel_id=1, replica_groups=mesh['own'=16,'red'=8] {'own'}, dimensions={0} | all-to-all | bytes 2048 | tf_op jit(solution)/shard_map/all_to_all | solution.py:51
  19.9 6.8 %copy_select_fusion = bf16[16,8,128,128]{3,1,2,0:T(8,128)(2,1)} fusion(bf16[16,8,128,128]{3,2,1,0:T(8,128)(2,1)} %bitcast.86, pred[16,8]{1,0:T(8,128)(4,1)S(1)} %copy.25), kind=kLoop, calls=%fused_computation.21 | loop fusion | flops 2097152 | bytes 8388736 | tf_op jit(solution)/shard_map/jit(_where)/select_n | solution.py:11
  26.7 4.7 %all-to-all-start.2 = ((bf16[16,8,128,128]{3,1,2,0:T(8,128)(2,1)}), bf16[16,8,128,128]{3,1,2,0:T(8,128)(2,1)}, u32[]{:S(2)}, u32[]{:S(2)}) async-start(bf16[16,8,128,128]{3,1,2,0:T(8,128)(2,1)} %copy_select_fusion), calls=%async_computation.2 | async-start | bytes 8388608 | tf_op jit(solution)/shard_map/all_to_all | solution.py:56
  31.8 3.0 gather_fusion
  34.8 6.8 %copy_select_fusion.1 = bf16[16,8,128,128]{3,1,2,0:T(8,128)(2,1)} fusion(bf16[16,8,128,128]{3,2,1,0:T(8,128)(2,1)} %bitcast.87, pred[16,8]{1,0:T(8,128)(4,1)S(1)} %copy.21), kind=kLoop, calls=%fused_computation.22 | loop fusion | flops 2097152 | bytes 8388736 | tf_op jit(solution)/shard_map/jit(_where)/select_n | solution.py:11
  41.7 44.4 %all-to-all-done.2 = bf16[16,8,128,128]{3,1,2,0:T(8,128)(2,1)} async-done(((bf16[16,8,128,128]{3,1,2,0:T(8,128)(2,1)}), bf16[16,8,128,128]{3,1,2,0:T(8,128)(2,1)}, u32[]{:S(2)}, u32[]{:S(2)}) %all-to-all-start.2) | async-done | bytes 4194336 | tf_op jit(solution)/shard_map/all_to_all | solution.py:56
  86.1 5.1 %all-to-all-start.1 = ((bf16[16,8,128,128]{3,1,2,0:T(8,128)(2,1)}), bf16[16,8,128,128]{3,1,2,0:T(8,128)(2,1)}, u32[]{:S(2)}, u32[]{:S(2)}) async-start(bf16[16,8,128,128]{3,1,2,0:T(8,128)(2,1)} %copy_select_fusion.1), calls=%async_computation.1 | async-start | bytes 8388608 | tf_op jit(solution)/shard_map/all_to_all | solution.py:55
  92.5 48.4 %all-to-all-done.1 = bf16[16,8,128,128]{3,1,2,0:T(8,128)(2,1)} async-done(((bf16[16,8,128,128]{3,1,2,0:T(8,128)(2,1)}), bf16[16,8,128,128]{3,1,2,0:T(8,128)(2,1)}, u32[]{:S(2)}, u32[]{:S(2)}) %all-to-all-start.1) | async-done | bytes 4194336 | tf_op jit(solution)/shard_map/all_to_all | solution.py:55
  140.9 178.0 %while.12 = (s32[]{:T(128)}, f32[4,8,128,128]{3,2,1,0:T(8,128)}, s32[4,8,64]{2,1,0:T(8,128)}, pred[4,8,64]{2,1,0:T(8,128)(4,1)S(1)}, bf16[128,16384]{1,0:T(8,128...) while((s32[]{:T(128)}, f32[4,8,128,128]{3,2,1,0:T(8,128)}, ...), condition=%wide.region_1.2_spmd.clone.clone, body=%wide.region_0.1_spmd.clone.clone.sunk | while | flops 6459424768 | bytes 143145056 | solution.py:45
  141.6 7.0 %convolution_convert_fusion.5 = bf16[8,64,16384]{2,1,0:T(8,128)(2,1)S(1)} fusion(bf16[128,16384]{1,0:T(8,128)(2,1)} %get-tuple-element.172, s32[8,64]{1,0:T(8,128)S(1)} %get-tuple-element.151, pred[8,64]{1,0:T(8,128)(4,1)S(1)} %dynamic-slice_bitcast_fusion.6), kind=kOutput, calls=%fused_computation.4.clone.1 | convolution fusion | flops 2156003328 | bytes 20974080 | tf_op jit(solution)/shard_map/while/body/eval_jaxpr/nkm,mx->nkx/dot_general | solution.py:30
  148.6 8.3 %copy.38 = bf16[64,8,128,128]{3,2,1,0:T(8,128)(2,1)} copy(bf16[64,8,128,128]{3,1,2,0:T(8,128)(2,1)S(1)} %bitcast.82) | data formatting | bytes 33554432 | tf_op jit(solution)/shard_map/while
  156.8 6.9 %convolution_convert_fusion.4 = bf16[8,64,16384]{2,1,0:T(8,128)(2,1)S(1)} fusion(bf16[128,16384]{1,0:T(8,128)(2,1)} %get-tuple-element.174, s32[8,64]{1,0:T(8,128)S(1)} %get-tuple-element.150), kind=kOutput, calls=%fused_computation.3.clone.1 | convolution fusion | flops 2155937792 | bytes 20973568 | tf_op jit(solution)/shard_map/while/body/eval_jaxpr/nkm,mx->nkx/dot_general | solution.py:33
  163.8 8.3 %copy.37 = bf16[64,8,128,128]{3,2,1,0:T(8,128)(2,1)} copy(bf16[64,8,128,128]{3,1,2,0:T(8,128)(2,1)S(1)} %bitcast.83) | data formatting | bytes 33554432 | tf_op jit(solution)/shard_map/while
  172.1 13.3 %fusion.30 = f32[4,8,128,128]{3,2,1,0:T(8,128)} fusion(f32[4,8,128,128]{3,2,1,0:T(8,128)} %get-tuple-element.161, s32[]{:T(128)} %get-tuple-element.160, bf16[8,64,128,128]{3,2,1,0:T(8,128)(2,1)} %bitcast.85, bf16[8,64,128,128]{3,2,1,0:T(8,128)(2,1)} %bitcast.84), kind=kOutput, calls=%fused_computation.11.clone.1 | convolution fusion | flops 2147483648 | bytes 34079232 | tf_op jit(solution)/shard_map/while/body/eval_jaxpr/nkpc,nkqc->npq/dot_general | solution.py:38
  186.1 7.0 %convolution_convert_fusion.5 = bf16[8,64,16384]{2,1,0:T(8,128)(2,1)S(1)} fusion(bf16[128,16384]{1,0:T(8,128)(2,1)} %get-tuple-element.172, s32[8,64]{1,0:T(8,128)S(1)} %get-tuple-element.151, pred[8,64]{1,0:T(8,128)(4,1)S(1)} %dynamic-slice_bitcast_fusion.6), kind=kOutput, calls=%fused_computation.4.clone.1 | convolution fusion | flops 2156003328 | bytes 20974080 | tf_op jit(solution)/shard_map/while/body/eval_jaxpr/nkm,mx->nkx/dot_general | solution.py:30
  193.0 8.3 %copy.38 = bf16[64,8,128,128]{3,2,1,0:T(8,128)(2,1)} copy(bf16[64,8,128,128]{3,1,2,0:T(8,128)(2,1)S(1)} %bitcast.82) | data formatting | bytes 33554432 | tf_op jit(solution)/shard_map/while
  201.3 6.9 %convolution_convert_fusion.4 = bf16[8,64,16384]{2,1,0:T(8,128)(2,1)S(1)} fusion(bf16[128,16384]{1,0:T(8,128)(2,1)} %get-tuple-element.174, s32[8,64]{1,0:T(8,128)S(1)} %get-tuple-element.150), kind=kOutput, calls=%fused_computation.3.clone.1 | convolution fusion | flops 2155937792 | bytes 20973568 | tf_op jit(solution)/shard_map/while/body/eval_jaxpr/nkm,mx->nkx/dot_general | solution.py:33
  208.3 8.3 %copy.37 = bf16[64,8,128,128]{3,2,1,0:T(8,128)(2,1)} copy(bf16[64,8,128,128]{3,1,2,0:T(8,128)(2,1)S(1)} %bitcast.83) | data formatting | bytes 33554432 | tf_op jit(solution)/shard_map/while
  216.6 13.3 %fusion.30 = f32[4,8,128,128]{3,2,1,0:T(8,128)} fusion(f32[4,8,128,128]{3,2,1,0:T(8,128)} %get-tuple-element.161, s32[]{:T(128)} %get-tuple-element.160, bf16[8,64,128,128]{3,2,1,0:T(8,128)(2,1)} %bitcast.85, bf16[8,64,128,128]{3,2,1,0:T(8,128)(2,1)} %bitcast.84), kind=kOutput, calls=%fused_computation.11.clone.1 | convolution fusion | flops 2147483648 | bytes 34079232 | tf_op jit(solution)/shard_map/while/body/eval_jaxpr/nkpc,nkqc->npq/dot_general | solution.py:38
  230.6 7.0 %convolution_convert_fusion.5 = bf16[8,64,16384]{2,1,0:T(8,128)(2,1)S(1)} fusion(bf16[128,16384]{1,0:T(8,128)(2,1)} %get-tuple-element.172, s32[8,64]{1,0:T(8,128)S(1)} %get-tuple-element.151, pred[8,64]{1,0:T(8,128)(4,1)S(1)} %dynamic-slice_bitcast_fusion.6), kind=kOutput, calls=%fused_computation.4.clone.1 | convolution fusion | flops 2156003328 | bytes 20974080 | tf_op jit(solution)/shard_map/while/body/eval_jaxpr/nkm,mx->nkx/dot_general | solution.py:30
  237.6 8.3 %copy.38 = bf16[64,8,128,128]{3,2,1,0:T(8,128)(2,1)} copy(bf16[64,8,128,128]{3,1,2,0:T(8,128)(2,1)S(1)} %bitcast.82) | data formatting | bytes 33554432 | tf_op jit(solution)/shard_map/while
  245.8 6.9 %convolution_convert_fusion.4 = bf16[8,64,16384]{2,1,0:T(8,128)(2,1)S(1)} fusion(bf16[128,16384]{1,0:T(8,128)(2,1)} %get-tuple-element.174, s32[8,64]{1,0:T(8,128)S(1)} %get-tuple-element.150), kind=kOutput, calls=%fused_computation.3.clone.1 | convolution fusion | flops 2155937792 | bytes 20973568 | tf_op jit(solution)/shard_map/while/body/eval_jaxpr/nkm,mx->nkx/dot_general | solution.py:33
  252.8 8.3 %copy.37 = bf16[64,8,128,128]{3,2,1,0:T(8,128)(2,1)} copy(bf16[64,8,128,128]{3,1,2,0:T(8,128)(2,1)S(1)} %bitcast.83) | data formatting | bytes 33554432 | tf_op jit(solution)/shard_map/while
  261.1 13.3 %fusion.30 = f32[4,8,128,128]{3,2,1,0:T(8,128)} fusion(f32[4,8,128,128]{3,2,1,0:T(8,128)} %get-tuple-element.161, s32[]{:T(128)} %get-tuple-element.160, bf16[8,64,128,128]{3,2,1,0:T(8,128)(2,1)} %bitcast.85, bf16[8,64,128,128]{3,2,1,0:T(8,128)(2,1)} %bitcast.84), kind=kOutput, calls=%fused_computation.11.clone.1 | convolution fusion | flops 2147483648 | bytes 34079232 | tf_op jit(solution)/shard_map/while/body/eval_jaxpr/nkpc,nkqc->npq/dot_general | solution.py:38
  275.1 7.0 %convolution_convert_fusion.5 = bf16[8,64,16384]{2,1,0:T(8,128)(2,1)S(1)} fusion(bf16[128,16384]{1,0:T(8,128)(2,1)} %get-tuple-element.172, s32[8,64]{1,0:T(8,128)S(1)} %get-tuple-element.151, pred[8,64]{1,0:T(8,128)(4,1)S(1)} %dynamic-slice_bitcast_fusion.6), kind=kOutput, calls=%fused_computation.4.clone.1 | convolution fusion | flops 2156003328 | bytes 20974080 | tf_op jit(solution)/shard_map/while/body/eval_jaxpr/nkm,mx->nkx/dot_general | solution.py:30
  282.1 8.3 %copy.38 = bf16[64,8,128,128]{3,2,1,0:T(8,128)(2,1)} copy(bf16[64,8,128,128]{3,1,2,0:T(8,128)(2,1)S(1)} %bitcast.82) | data formatting | bytes 33554432 | tf_op jit(solution)/shard_map/while
  290.4 6.9 %convolution_convert_fusion.4 = bf16[8,64,16384]{2,1,0:T(8,128)(2,1)S(1)} fusion(bf16[128,16384]{1,0:T(8,128)(2,1)} %get-tuple-element.174, s32[8,64]{1,0:T(8,128)S(1)} %get-tuple-element.150), kind=kOutput, calls=%fused_computation.3.clone.1 | convolution fusion | flops 2155937792 | bytes 20973568 | tf_op jit(solution)/shard_map/while/body/eval_jaxpr/nkm,mx->nkx/dot_general | solution.py:33
  297.3 8.3 %copy.37 = bf16[64,8,128,128]{3,2,1,0:T(8,128)(2,1)} copy(bf16[64,8,128,128]{3,1,2,0:T(8,128)(2,1)S(1)} %bitcast.83) | data formatting | bytes 33554432 | tf_op jit(solution)/shard_map/while
  305.6 13.3 %fusion.30 = f32[4,8,128,128]{3,2,1,0:T(8,128)} fusion(f32[4,8,128,128]{3,2,1,0:T(8,128)} %get-tuple-element.161, s32[]{:T(128)} %get-tuple-element.160, bf16[8,64,128,128]{3,2,1,0:T(8,128)(2,1)} %bitcast.85, bf16[8,64,128,128]{3,2,1,0:T(8,128)(2,1)} %bitcast.84), kind=kOutput, calls=%fused_computation.11.clone.1 | convolution fusion | flops 2147483648 | bytes 34079232 | tf_op jit(solution)/shard_map/while/body/eval_jaxpr/nkpc,nkqc->npq/dot_general | solution.py:38
  318.9 4.4 %collective-permute-done = f32[32,128,128]{2,1,0:T(8,128)S(1)} collective-permute-done((f32[32,128,128]{2,1,0:T(8,128)}, f32[32,128,128]{2,1,0:T(8,128)S(1)}, u32[]{:S(2)}, u32[]{:S(2)}) %collective-permute-start) | collective-permute-done | bytes 2097184 | tf_op jit(solution)/shard_map/ppermute | solution.py:67
  326.9 46.2 %collective-permute-done.1 = f32[32,128,128]{2,1,0:T(8,128)S(1)} collective-permute-done((f32[32,128,128]{2,1,0:T(8,128)S(1)}, f32[32,128,128]{2,1,0:T(8,128)S(1)}, u32[]{:S(2)}, u32[]{:S(2)}) %collective-permute-start.1) | collective-permute-done | bytes 2097184 | tf_op jit(solution)/shard_map/ppermute | solution.py:67
  377.7 45.6 %collective-permute-done.2 = f32[32,128,128]{2,1,0:T(8,128)} collective-permute-done((f32[32,128,128]{2,1,0:T(8,128)}, f32[32,128,128]{2,1,0:T(8,128)}, u32[]{:S(2)}, u32[]{:S(2)}) %collective-permute-start.2) | collective-permute-done | bytes 2097184 | tf_op jit(solution)/shard_map/ppermute | solution.py:67
  (44 shorter events, 18.7 us)
Async XLA Ops:
  0.0 16.8 %copy-start = (bf16[64,128,128]{2,1,0:T(8,128)(2,1)S(1)}, bf16[64,128,128]{2,1,0:T(8,128)(2,1)}, u32[]{:S(2)}) copy-start(bf16[64,128,128]{2,1,0:T(8,128)(2,1)} %param.9) | copy-start | bytes 6291460
  26.7 5.0 %copy-start.2 = (bf16[64,128,128]{2,1,0:T(8,128)(2,1)S(1)}, bf16[64,128,128]{2,1,0:T(8,128)(2,1)}, u32[]{:S(2)}) copy-start(bf16[64,128,128]{2,1,0:T(8,128)(2,1)} %param.8) | copy-start | bytes 6291460
  26.7 59.3 %all-to-all-start.2 = ((bf16[16,8,128,128]{3,1,2,0:T(8,128)(2,1)}), bf16[16,8,128,128]{3,1,2,0:T(8,128)(2,1)}, u32[]{:S(2)}, u32[]{:S(2)}) async-start(bf16[16,8,128,128]{3,1,2,0:T(8,128)(2,1)} %copy_select_fusion), calls=%async_computation.2 | async-start | bytes 8388608 | tf_op jit(solution)/shard_map/all_to_all | solution.py:56
  41.7 50.0 %copy-start.3 = (s32[32,1]{0,1:T(1,128)S(1)}, s32[32,1]{0,1:T(1,128)}, u32[]{:S(2)}) copy-start(s32[32,1]{0,1:T(1,128)} %param.13) | copy-start | bytes 388
  86.1 54.8 %all-to-all-start.1 = ((bf16[16,8,128,128]{3,1,2,0:T(8,128)(2,1)}), bf16[16,8,128,128]{3,1,2,0:T(8,128)(2,1)}, u32[]{:S(2)}, u32[]{:S(2)}) async-start(bf16[16,8,128,128]{3,1,2,0:T(8,128)(2,1)} %copy_select_fusion.1), calls=%async_computation.1 | async-start | bytes 8388608 | tf_op jit(solution)/shard_map/all_to_all | solution.py:55
  318.9 4.4 %collective-permute-start = (f32[32,128,128]{2,1,0:T(8,128)}, f32[32,128,128]{2,1,0:T(8,128)S(1)}, u32[]{:S(2)}, u32[]{:S(2)}) collective-permute-start(f32[32,128,128]{2,1,0:T(8,128)} %bitcast.88), channel_id=1, source_target_pairs={{0,1},{1,0},{2,3},{3,2},{4,5},{5,4},{6,7},{7,6},{8,9},{9,8},{10,11... | collective-permute-start | bytes 6291464 | tf_op jit(solution)/shard_map/ppermute | solution.py:67
  323.3 101.8 %copy-start.1 = (bf16[64,128,128]{2,1,0:T(8,128)(2,1)S(1)}, bf16[64,128,128]{2,1,0:T(8,128)(2,1)}, u32[]{:S(2)}) copy-start(bf16[64,128,128]{2,1,0:T(8,128)(2,1)} %param.9) | copy-start | bytes 6291460
  325.3 47.8 %collective-permute-start.1 = (f32[32,128,128]{2,1,0:T(8,128)S(1)}, f32[32,128,128]{2,1,0:T(8,128)S(1)}, u32[]{:S(2)}, u32[]{:S(2)}) collective-permute-start(f32[32,128,128]{2,1,0:T(8,128)S(1)} %bitcast_add_fusion), channel_id=1, source_target_pairs={{0,2},{1,3},{2,0},{3,1},{4,6},{5,7},{6,4},{7,5},{8,10},{9,11},{10,... | collective-permute-start | bytes 6291464 | tf_op jit(solution)/shard_map/ppermute | solution.py:67
  374.7 48.6 %collective-permute-start.2 = (f32[32,128,128]{2,1,0:T(8,128)}, f32[32,128,128]{2,1,0:T(8,128)}, u32[]{:S(2)}, u32[]{:S(2)}) collective-permute-start(f32[32,128,128]{2,1,0:T(8,128)} %add.38), channel_id=1, source_target_pairs={{0,4},{1,5},{2,6},{3,7},{4,0},{5,1},{6,2},{7,3},{8,12},{9,13},{10,... | collective-permute-start | bytes 6291464 | tf_op jit(solution)/shard_map/ppermute | solution.py:67
